TPU v7x, 256 devices: a whole 4x4x8 slice. The times are simulated.
256 devices in a mesh: aux: 16 (over x, y), occ: 16 (over z, core).
Axes of the slice: x: 4, y: 4, z: 8, core: 2. Of those that a mesh axis runs over, the one named last changes fastest.
Arguments:
- integrals: bfloat16 [32, 384, 128, 128], P('aux', 'occ'), may hold values from -1.5 to 1.5
- coefficients: bfloat16 [4096, 384], P('occ'), may hold values from -0.21875 to 0.21875
- pair_rows: int32 [16, 384], P('aux', 'occ'), may hold values from 0 to 1
- pair_cols: int32 [16, 384], P('aux', 'occ'), may hold values from 0 to 31
- pair_count: int32 [16, 16], P('aux', 'occ'), may hold values from 1 to 24, as said below
- row_blocks: int32 [32], replicated, may hold values from 0 to 31, each once
Outputs:
- exchange_matrix: float32 [4096, 4096], P('aux', 'occ')
Inputs may be any that keep to these rules, and one draw needn't show every extreme that they name: `pair_count`: at most 24 live slots for each auxiliary block and row owner, and some auxiliary block and owner has exactly 24.
All inputs are finite; a program needn't handle non-finite values.
Results may differ from a plain program's by a relative error of at most 0.0022.
Values may be sent and summed in bfloat16 or wider, within the bound.
A program may use at most 64 MiB of HBM per device.

v0:
```python
import jax
import jax.numpy as jnp
from jax import lax
from jax.sharding import PartitionSpec as P


def contract_rows(first, second):
    return jnp.einsum("pni,pmi->nm", first, second, preferred_element_type=jnp.float32)


def local(integrals, coefficients, pair_rows, pair_cols, pair_count, row_blocks):
    aux_count = integrals.shape[0]
    block_size = integrals.shape[2]
    block_total = row_blocks.shape[0]
    occ_size = lax.axis_size("occ")
    own_blocks = block_total // occ_size
    strip_width = own_blocks * block_size
    full_coeff = lax.all_gather(coefficients, "occ", axis=0, tiled=True)
    orbitals = full_coeff.shape[1]
    coeff_blocks = full_coeff.reshape(block_total, block_size, orbitals)

    def add_pair(slot_index, partial_half):
        row_slot = pair_rows[0, slot_index]
        basis_block = row_blocks[pair_cols[0, slot_index]]
        coeff_piece = lax.dynamic_index_in_dim(coeff_blocks, basis_block, 0, keepdims=False)
        integral_piece = lax.dynamic_index_in_dim(integrals, slot_index, 1, keepdims=False)
        product = jnp.einsum(
            "pmn,ni->pmi", integral_piece, coeff_piece, preferred_element_type=jnp.float32
        )
        current = lax.dynamic_index_in_dim(partial_half, row_slot, 1, keepdims=False)
        return lax.dynamic_update_index_in_dim(partial_half, current + product, row_slot, 1)

    start_half = jnp.zeros((aux_count, own_blocks, block_size, orbitals), jnp.float32)
    summed_half = lax.fori_loop(0, pair_count[0, 0], add_pair, start_half)
    half = summed_half.reshape(aux_count, strip_width, orbitals).astype(jnp.bfloat16)
    strip = contract_rows(lax.all_gather(half, "occ", axis=1, tiled=True), half)
    summed = lax.psum(strip, "aux")
    share_rows = summed.shape[0] // lax.axis_size("aux")
    mine = lax.dynamic_slice_in_dim(summed, lax.axis_index("aux") * share_rows, share_rows, 0)
    return mine


def solution(mesh):
    return jax.shard_map(
        local,
        mesh=mesh,
        in_specs=(
            P("aux", "occ", None, None),
            P("occ", None),
            P("aux", "occ"),
            P("aux", "occ"),
            P("aux", "occ"),
            P(),
        ),
        out_specs=P("aux", "occ"),
        check_vma=False,
    )
```

profile of v0, /device:TPU:1, one launch (start us, length us, event | category | flops | bytes accessed | tf_op | source)
XLA Modules:
  0.0 470.6 jit_solution(8826988646007465637)
XLA Ops:
  7.3 47.1 %all-gather.3.cloned.1.call-done = bf16[4096,384]{1,0:T(8,128)(2,1)} async-done(((bf16[256,384]{1,0:T(8,128)(2,1)}), bf16[4096,384]{1,0:T(8,128)(2,1)}) %all-gather.3.cloned.1.call-update) | async-done | bytes 3145744 | tf_op jit(solution)/shard_map/all_gather | solution.py:18
  54.5 142.6 %while.10 = (s32[]{:T(128)}, f32[2,2,128,384]{3,2,0,1:T(8,128)S(1)}, s32[]{:T(128)}, s32[1,24]{1,0:T(1,128)}, bf16[2,24,128,128]{3,2,1,0:T(8,128)(2,1)}, /*index...) while((s32[]{:T(128)}, ...), condition=%wide.region_1.2_spmd, body=%wide.region_0.1_spmd.sunk | while | flops 25264140 | bytes 1737021 | solution.py:34
  55.1 1.3 constant_dynamic-slice_fusion.6
  60.3 1.3 dynamic_slice.46
  63.5 1.1 fusion.14
  65.3 1.3 constant_dynamic-slice_fusion.6
  70.4 1.3 dynamic_slice.46
  73.6 1.1 fusion.14
  75.4 1.3 constant_dynamic-slice_fusion.6
  80.6 1.3 dynamic_slice.46
  83.7 1.1 fusion.14
  85.6 1.3 constant_dynamic-slice_fusion.6
  90.7 1.3 dynamic_slice.46
  93.9 1.1 fusion.14
  95.7 1.3 constant_dynamic-slice_fusion.6
  100.8 1.3 dynamic_slice.46
  104.0 1.1 fusion.14
  105.8 1.3 constant_dynamic-slice_fusion.6
  111.0 1.3 dynamic_slice.46
  114.2 1.1 fusion.14
  116.0 1.3 constant_dynamic-slice_fusion.6
  121.1 1.3 dynamic_slice.46
  124.3 1.1 fusion.14
  126.1 1.3 constant_dynamic-slice_fusion.6
  131.3 1.3 dynamic_slice.46
  134.4 1.1 fusion.14
  136.3 1.3 constant_dynamic-slice_fusion.6
  141.4 1.3 dynamic_slice.46
  144.6 1.1 fusion.14
  146.4 1.3 constant_dynamic-slice_fusion.6
  151.6 1.3 dynamic_slice.46
  154.7 1.1 fusion.14
  156.5 1.3 constant_dynamic-slice_fusion.6
  161.7 1.3 dynamic_slice.46
  164.9 1.1 fusion.14
  166.7 1.3 constant_dynamic-slice_fusion.6
  171.8 1.3 dynamic_slice.46
  175.0 1.1 fusion.14
  176.8 1.3 constant_dynamic-slice_fusion.6
  182.0 1.3 dynamic_slice.46
  185.1 1.1 fusion.14
  187.0 1.3 constant_dynamic-slice_fusion.6
  192.1 1.3 dynamic_slice.46
  195.3 1.1 fusion.14
  198.0 145.8 %all-gather.5.cloned.1.call-done = bf16[2,4096,384]{2,1,0:T(8,128)(2,1)} async-done(((bf16[2,256,384]{2,1,0:T(8,128)(2,1)}), bf16[2,4096,384]{2,1,0:T(8,128)(2,1)}) %all-gather.5.cloned.1.call-update) | async-done | bytes 6291472 | tf_op jit(solution)/shard_map/all_gather | solution.py:36
  343.8 6.7 %convolution_bitcast_fusion = f32[4096,256]{1,0:T(8,128)} fusion(bf16[2,4096,384]{2,1,0:T(8,128)(2,1)} %all-gather.5.cloned.1.call-done, bf16[2,256,384]{2,1,0:T(8,128)(2,1)} %bitcast.40), kind=kOutput, calls=%fused_computation.11 | convolution fusion | flops 1610612736 | bytes 10878976 | tf_op jit(solution)/shard_map/pni,pmi->nm/dot_general | solution.py:8
  350.5 111.8 %all-reduce.2.cloned.1.call-done = f32[4096,256]{1,0:T(8,128)} async-done(((f32[4096,256]{1,0:T(8,128)}), f32[4096,256]{1,0:T(8,128)}) %all-reduce.2.cloned.1.call-update) | async-done | bytes 4194320 | tf_op jit(solution)/shard_map/psum | solution.py:37
  462.4 1.7 constant_dynamic-slice_fusion.3
  (23 shorter events, 2.2 us)
Async XLA Ops:
  6.5 47.9 %all-gather.3.cloned.1.call-start = ((), (), s32[]{:S(2)}) async-start(), calls=%async_computation | async-start | bytes 3342336 | tf_op jit(solution)/shard_map/all_gather | solution.py:18
  7.3 336.6 %all-gather.5.cloned.1.call-start = ((), (), s32[]{:S(2)}) async-start(), calls=%async_computation.1 | async-start | bytes 6684672 | tf_op jit(solution)/shard_map/all_gather | solution.py:36
  198.0 264.4 %all-reduce.2.cloned.1.call-start = ((), (), s32[]{:S(2)}) async-start(), calls=%async_computation.2 | async-start | bytes 8388608 | tf_op jit(solution)/shard_map/psum | solution.py:37
Sparse Core Ops, SparseCore 0:
  9.2 45.1 all-gather.2
  198.1 145.6 all-gather.4
  350.6 111.6 all-reduce.1
where the time goes:
time: 474 us; the launch traced here: 471 us
  waiting for transfers between devices  305 us (64%)
  loops' own time  90.1 us (19%)
  local copies, waits for them, and re-layouts  39.1 us (8%)
  matrix products  22.6 us (5%)
  between operations  13.1 us (3%)
    all_gather x1, waiting for transfers between devices, local(): strip = contract_rows(lax.all_gather(half, 'occ', axis=1, tiled=True), half)  146 us
    psum x1, waiting for transfers between devices, local(): summed = lax.psum(strip, 'aux')  112 us
    another operation x1, loops' own time, local(): summed_half = lax.fori_loop(0, pair_count[0, 0], add_pair, start_half)  90.1 us
    all_gather x1, waiting for transfers between devices, local(): full_coeff = lax.all_gather(coefficients, 'occ', axis=0, tiled=True)  47.1 us
    dynamic_slice x28, local copies, waits for them, and re-layouts, add_pair(): basis_block = row_blocks[pair_cols[0, slot_index]]  36.1 us
    dot_general x14, matrix products, add_pair(): jnp.einsum('pmn,ni->pmi', integral_piece, coeff_piece, preferred_element_...  15.9 us
  transfers between devices with their start and end apart: 3, of which 3 were waited for; matrix products, arithmetic and copies ran while one was open for 0% of the time, Pallas kernels for 0%

commit v1 on v0

--- a/solution.py
+++ b/solution.py
@@ -1,7 +1,33 @@
+import functools
 import jax
 import jax.numpy as jnp
 from jax import lax
 from jax.sharding import PartitionSpec as P
+from jax.lax import axis_index, axis_size, ppermute
+
+
+def wall_supply(t0, dim_at):
+    placed, s_next, mat_out = (axis_size("occ"), axis_index("occ"), t0.shape[dim_at])
+    items = [(pp, (pp + 1) % placed) for pp in range(placed)]
+    series = [(pp, (pp - 1) % placed) for pp in range(placed)]
+    z = jnp.zeros((*t0.shape[:dim_at], placed * mat_out, *t0.shape[dim_at + 1 :]), t0.dtype)
+    z = lax.dynamic_update_slice_in_dim(z, t0, s_next * mat_out, axis=dim_at)
+    mid_arr = formed = t0
+    n_now = placed // 2
+    for to_i in range(1, n_now + 1):
+        mid_arr = ppermute(mid_arr, "occ", items)
+        z = lax.dynamic_update_slice_in_dim(
+            z, mid_arr, (s_next - to_i) % placed * mat_out, axis=dim_at
+        )
+        if to_i < placed - n_now:
+            formed = ppermute(formed, "occ", series)
+            z = lax.dynamic_update_slice_in_dim(
+                z, formed, (s_next + to_i) % placed * mat_out, axis=dim_at
+            )
+    return z
+
+
+_apply_paths = functools.partial(wall_supply, dim_at=1)
 
 
 def contract_rows(first, second):
@@ -33,7 +59,7 @@
     start_half = jnp.zeros((aux_count, own_blocks, block_size, orbitals), jnp.float32)
     summed_half = lax.fori_loop(0, pair_count[0, 0], add_pair, start_half)
     half = summed_half.reshape(aux_count, strip_width, orbitals).astype(jnp.bfloat16)
-    strip = contract_rows(lax.all_gather(half, "occ", axis=1, tiled=True), half)
+    strip = contract_rows(_apply_paths(half), half)
     summed = lax.psum(strip, "aux")
     share_rows = summed.shape[0] // lax.axis_size("aux")
     mine = lax.dynamic_slice_in_dim(summed, lax.axis_index("aux") * share_rows, share_rows, 0)

time: 474 us -> 480 us (1.013)
  starting transfers between devices: 0.08 us -> 107 us
  waiting for transfers between devices: 305 us -> 210 us
    all_gather x1 -> x0, waiting for transfers between devices: 146 us -> none  [local(): strip = contract_rows(lax.all_gather(half, 'occ', axis=1, tiled=True), half)]
    ppermute x0 -> x15, starting transfers between devices: none -> 107 us  [the longest x8 62.5 us: wall_supply(): mid_arr = ppermute(mid_arr, 'occ', items)]
    psum x1, waiting for transfers between devices: 112 us -> 143 us  [local(): summed = lax.psum(strip, 'aux')]
    ppermute x0 -> x15, waiting for transfers between devices: none -> 19.1 us  [the longest x8 16.1 us: wall_supply(): mid_arr = ppermute(mid_arr, 'occ', items)]
  transfers between devices with their start and end apart: 3 -> 17, of which waited for: 3 -> 15; matrix products, arithmetic and copies ran while one was open for 0% -> 0% of each run, Pallas kernels for 0% -> 0%
where the time goes in v1:
time: 480 us; the launch traced here: 476 us
  waiting for transfers between devices  210 us (44%)
  starting transfers between devices  107 us (22%)
  loops' own time  86.2 us (18%)
  local copies, waits for them, and re-layouts  39.6 us (8%)
  matrix products  19.8 us (4%)
  between operations  13.5 us (3%)
    psum x1, waiting for transfers between devices, local(): summed = lax.psum(strip, 'aux')  143 us
    another operation x1, loops' own time, local(): summed_half = lax.fori_loop(0, pair_count[0, 0], add_pair, start_half)  86.2 us
    ppermute x8, starting transfers between devices, wall_supply(): mid_arr = ppermute(mid_arr, 'occ', items)  62.5 us
    all_gather x1, waiting for transfers between devices, local(): full_coeff = lax.all_gather(coefficients, 'occ', axis=0, tiled=True)  47.1 us
    ppermute x7, starting transfers between devices, wall_supply(): formed = ppermute(formed, 'occ', series)  44.2 us
    dynamic_slice x28, local copies, waits for them, and re-layouts, add_pair(): basis_block = row_blocks[pair_cols[0, slot_index]]  35.5 us
    ppermute x8, waiting for transfers between devices, wall_supply(): mid_arr = ppermute(mid_arr, 'occ', items)  16.1 us
    dot_general x14, matrix products, add_pair(): jnp.einsum('pmn,ni->pmi', integral_piece, coeff_piece, preferred_element_...  15.9 us
  transfers between devices with their start and end apart: 17, of which 15 were waited for; matrix products, arithmetic and copies ran while one was open for 0% of the time, Pallas kernels for 0%

profile of v1, /device:TPU:1, one launch (start us, length us, event | category | flops | bytes accessed | tf_op | source)
XLA Modules:
  0.0 476.2 jit_solution(13779007367232960431)
XLA Ops:
  7.3 47.1 %all-gather.2.cloned.1.call-done = bf16[4096,384]{1,0:T(8,128)(2,1)} async-done(((bf16[256,384]{1,0:T(8,128)(2,1)}), bf16[4096,384]{1,0:T(8,128)(2,1)}) %all-gather.2.cloned.1.call-update) | async-done | bytes 3145744 | tf_op jit(solution)/shard_map/all_gather | solution.py:44
  54.5 138.1 %while.10 = (s32[]{:T(128)}, f32[2,2,128,384]{3,2,1,0:T(8,128)S(1)}, s32[]{:T(128)}, s32[1,24]{1,0:T(1,128)}, bf16[2,24,128,128]{3,2,1,0:T(8,128)(2,1)}, /*index...) while((s32[]{:T(128)}, ...), condition=%wide.region_1.2_spmd, body=%wide.region_0.1_spmd.sunk | while | flops 25264140 | bytes 1737013 | solution.py:60
  55.1 1.3 constant_dynamic-slice_fusion.6
  60.0 1.3 dynamic_slice.46
  63.1 1.1 fusion.14
  65.0 1.3 constant_dynamic-slice_fusion.6
  69.8 1.3 dynamic_slice.46
  74.8 1.3 constant_dynamic-slice_fusion.6
  79.7 1.3 dynamic_slice.46
  84.6 1.3 constant_dynamic-slice_fusion.6
  89.5 1.3 dynamic_slice.46
  94.4 1.3 constant_dynamic-slice_fusion.6
  99.3 1.3 dynamic_slice.46
  104.2 1.3 constant_dynamic-slice_fusion.6
  109.1 1.3 dynamic_slice.46
  114.1 1.3 constant_dynamic-slice_fusion.6
  118.9 1.3 dynamic_slice.46
  123.9 1.3 constant_dynamic-slice_fusion.6
  128.8 1.3 dynamic_slice.46
  133.7 1.3 constant_dynamic-slice_fusion.6
  138.6 1.3 dynamic_slice.46
  141.7 1.1 fusion.14
  143.5 1.3 constant_dynamic-slice_fusion.6
  148.4 1.3 dynamic_slice.46
  153.3 1.3 constant_dynamic-slice_fusion.6
  158.2 1.3 dynamic_slice.46
  163.1 1.3 constant_dynamic-slice_fusion.6
  168.0 1.3 dynamic_slice.46
  173.0 1.3 constant_dynamic-slice_fusion.6
  177.8 1.3 dynamic_slice.46
  182.8 1.3 constant_dynamic-slice_fusion.6
  187.7 1.3 dynamic_slice.46
  192.6 60.0 %collective-permute-start = (bf16[2,256,384]{2,1,0:T(8,128)(2,1)S(1)}, bf16[2,256,384]{2,1,0:T(8,128)(2,1)S(1)}, u32[]{:S(2)}, u32[]{:S(2)}) collective-permute-start(bf16[2,256,384]{2,1,0:T(8,128)(2,1)S(1)} %bitcast.43), channel_id=1, source_target_pairs={{0,1},{1,2},{2,3},{3,4},{4,5},{5,6},{6,7},{7,8},{8,9},{9,10},{10,1... | collective-permute-start | bytes 1179656 | tf_op jit(solution)/shard_map/ppermute | solution.py:18
  252.7 4.7 collective-permute-done
  257.4 2.5 collective-permute-start.2
  259.9 8.9 %collective-permute-start.3 = (bf16[2,256,384]{2,1,0:T(8,128)(2,1)S(1)}, bf16[2,256,384]{2,1,0:T(8,128)(2,1)S(1)}, u32[]{:S(2)}, u32[]{:S(2)}) collective-permute-start(bf16[2,256,384]{2,1,0:T(8,128)(2,1)S(1)} %collective-permute-done.1), channel_id=1, source_target_pairs={{0,15},{1,0},{2,1},{3,2},{4,3},{5,4},{6,5},{7,6},{8,7},{9,8},{10,9... | collective-permute-start | bytes 1179656 | tf_op jit(solution)/shard_map/ppermute | solution.py:23
  268.8 1.2 collective-permute-done.2
  270.2 7.0 %collective-permute-start.5 = (bf16[2,256,384]{2,1,0:T(8,128)(2,1)S(1)}, bf16[2,256,384]{2,1,0:T(8,128)(2,1)S(1)}, u32[]{:S(2)}, u32[]{:S(2)}) collective-permute-start(bf16[2,256,384]{2,1,0:T(8,128)(2,1)S(1)} %collective-permute-done.3), channel_id=1, source_target_pairs={{0,15},{1,0},{2,1},{3,2},{4,3},{5,4},{6,5},{7,6},{8,7},{9,8},{10,9... | collective-permute-start | bytes 1179656 | tf_op jit(solution)/shard_map/ppermute | solution.py:23
  277.2 1.2 collective-permute-done.4
  278.6 7.1 %collective-permute-start.7 = (bf16[2,256,384]{2,1,0:T(8,128)(2,1)S(1)}, bf16[2,256,384]{2,1,0:T(8,128)(2,1)S(1)}, u32[]{:S(2)}, u32[]{:S(2)}) collective-permute-start(bf16[2,256,384]{2,1,0:T(8,128)(2,1)S(1)} %collective-permute-done.5), channel_id=1, source_target_pairs={{0,15},{1,0},{2,1},{3,2},{4,3},{5,4},{6,5},{7,6},{8,7},{9,8},{10,9... | collective-permute-start | bytes 1179656 | tf_op jit(solution)/shard_map/ppermute | solution.py:23
  285.6 1.2 collective-permute-done.6
  287.9 7.2 %collective-permute-start.9 = (bf16[2,256,384]{2,1,0:T(8,128)(2,1)S(1)}, bf16[2,256,384]{2,1,0:T(8,128)(2,1)S(1)}, u32[]{:S(2)}, u32[]{:S(2)}) collective-permute-start(bf16[2,256,384]{2,1,0:T(8,128)(2,1)S(1)} %collective-permute-done.7), channel_id=1, source_target_pairs={{0,15},{1,0},{2,1},{3,2},{4,3},{5,4},{6,5},{7,6},{8,7},{9,8},{10,9... | collective-permute-start | bytes 1179656 | tf_op jit(solution)/shard_map/ppermute | solution.py:23
  296.5 6.9 %collective-permute-start.11 = (bf16[2,256,384]{2,1,0:T(8,128)(2,1)S(1)}, bf16[2,256,384]{2,1,0:T(8,128)(2,1)S(1)}, u32[]{:S(2)}, u32[]{:S(2)}) collective-permute-start(bf16[2,256,384]{2,1,0:T(8,128)(2,1)S(1)} %collective-permute-done.9), channel_id=1, source_target_pairs={{0,15},{1,0},{2,1},{3,2},{4,3},{5,4},{6,5},{7,6},{8,7},{9,8},{10,9... | collective-permute-start | bytes 1179656 | tf_op jit(solution)/shard_map/ppermute | solution.py:23
  304.7 7.1 %collective-permute-start.13 = (bf16[2,256,384]{2,1,0:T(8,128)(2,1)S(1)}, bf16[2,256,384]{2,1,0:T(8,128)(2,1)S(1)}, u32[]{:S(2)}, u32[]{:S(2)}) collective-permute-start(bf16[2,256,384]{2,1,0:T(8,128)(2,1)S(1)} %collective-permute-done.11), channel_id=1, source_target_pairs={{0,15},{1,0},{2,1},{3,2},{4,3},{5,4},{6,5},{7,6},{8,7},{9,8},{10,9... | collective-permute-start | bytes 1179656 | tf_op jit(solution)/shard_map/ppermute | solution.py:23
  313.2 7.3 %collective-permute-done.14 = bf16[2,256,384]{2,1,0:T(8,128)(2,1)S(1)} collective-permute-done((bf16[2,256,384]{2,1,0:T(8,128)(2,1)S(1)}, bf16[2,256,384]{2,1,0:T(8,128)(2,1)S(1)}, u32[]{:S(2)}, u32[]{:S(2)}) %collective-permute-start.14) | collective-permute-done | bytes 393248 | tf_op jit(solution)/shard_map/ppermute | solution.py:18
  320.6 3.9 convolution_bitcast_fusion
  324.5 143.3 %all-reduce.2.cloned.1.call-done = f32[4096,256]{1,0:T(8,128)} async-done(((f32[4096,256]{1,0:T(8,128)}), f32[4096,256]{1,0:T(8,128)}) %all-reduce.2.cloned.1.call-update) | async-done | bytes 4194320 | tf_op jit(solution)/shard_map/psum | solution.py:63
  467.7 1.7 constant_dynamic-slice_fusion.3
  (70 shorter events, 20.4 us)
Async XLA Ops:
  6.5 47.9 %all-gather.2.cloned.1.call-start = ((), (), s32[]{:S(2)}) async-start(), calls=%async_computation | async-start | bytes 3342336 | tf_op jit(solution)/shard_map/all_gather | solution.py:44
  7.3 460.5 %all-reduce.2.cloned.1.call-start = ((), (), s32[]{:S(2)}) async-start(), calls=%async_computation.1 | async-start | bytes 8388608 | tf_op jit(solution)/shard_map/psum | solution.py:63
  192.6 64.8 %collective-permute-start = (bf16[2,256,384]{2,1,0:T(8,128)(2,1)S(1)}, bf16[2,256,384]{2,1,0:T(8,128)(2,1)S(1)}, u32[]{:S(2)}, u32[]{:S(2)}) collective-permute-start(bf16[2,256,384]{2,1,0:T(8,128)(2,1)S(1)} %bitcast.43), channel_id=1, source_target_pairs={{0,1},{1,2},{2,3},{3,4},{4,5},{5,6},{6,7},{7,8},{8,9},{9,10},{10,1... | collective-permute-start | bytes 1179656 | tf_op jit(solution)/shard_map/ppermute | solution.py:18
  252.7 7.2 %collective-permute-start.1 = (bf16[2,256,384]{2,1,0:T(8,128)(2,1)S(1)}, bf16[2,256,384]{2,1,0:T(8,128)(2,1)S(1)}, u32[]{:S(2)}, u32[]{:S(2)}) collective-permute-start(bf16[2,256,384]{2,1,0:T(8,128)(2,1)S(1)} %bitcast.44), channel_id=1, source_target_pairs={{0,15},{1,0},{2,1},{3,2},{4,3},{5,4},{6,5},{7,6},{8,7},{9,8},{10,9... | collective-permute-start | bytes 1179656 | tf_op jit(solution)/shard_map/ppermute | solution.py:23
  257.4 19.8 %copy-start = (bf16[2,256,384]{2,1,0:T(8,128)(2,1)}, bf16[2,256,384]{2,1,0:T(8,128)(2,1)S(1)}, u32[]{:S(2)}) copy-start(bf16[2,256,384]{2,1,0:T(8,128)(2,1)S(1)} %collective-permute-done) | copy-start | bytes 1179652
  257.4 12.6 %collective-permute-start.2 = (bf16[2,256,384]{2,1,0:T(8,128)(2,1)S(1)}, bf16[2,256,384]{2,1,0:T(8,128)(2,1)S(1)}, u32[]{:S(2)}, u32[]{:S(2)}) collective-permute-start(bf16[2,256,384]{2,1,0:T(8,128)(2,1)S(1)} %collective-permute-done), channel_id=1, source_target_pairs={{0,1},{1,2},{2,3},{3,4},{4,5},{5,6},{6,7},{7,8},{8,9},{9,10},{10,1... | collective-permute-start | bytes 1179656 | tf_op jit(solution)/shard_map/ppermute | solution.py:18
  259.9 10.3 %collective-permute-start.3 = (bf16[2,256,384]{2,1,0:T(8,128)(2,1)S(1)}, bf16[2,256,384]{2,1,0:T(8,128)(2,1)S(1)}, u32[]{:S(2)}, u32[]{:S(2)}) collective-permute-start(bf16[2,256,384]{2,1,0:T(8,128)(2,1)S(1)} %collective-permute-done.1), channel_id=1, source_target_pairs={{0,15},{1,0},{2,1},{3,2},{4,3},{5,4},{6,5},{7,6},{8,7},{9,8},{10,9... | collective-permute-start | bytes 1179656 | tf_op jit(solution)/shard_map/ppermute | solution.py:23
  270.0 8.4 %collective-permute-start.4 = (bf16[2,256,384]{2,1,0:T(8,128)(2,1)S(1)}, bf16[2,256,384]{2,1,0:T(8,128)(2,1)S(1)}, u32[]{:S(2)}, u32[]{:S(2)}) collective-permute-start(bf16[2,256,384]{2,1,0:T(8,128)(2,1)S(1)} %collective-permute-done.2), channel_id=1, source_target_pairs={{0,1},{1,2},{2,3},{3,4},{4,5},{5,6},{6,7},{7,8},{8,9},{9,10},{10,1... | collective-permute-start | bytes 1179656 | tf_op jit(solution)/shard_map/ppermute | solution.py:18
  270.2 8.4 %collective-permute-start.5 = (bf16[2,256,384]{2,1,0:T(8,128)(2,1)S(1)}, bf16[2,256,384]{2,1,0:T(8,128)(2,1)S(1)}, u32[]{:S(2)}, u32[]{:S(2)}) collective-permute-start(bf16[2,256,384]{2,1,0:T(8,128)(2,1)S(1)} %collective-permute-done.3), channel_id=1, source_target_pairs={{0,15},{1,0},{2,1},{3,2},{4,3},{5,4},{6,5},{7,6},{8,7},{9,8},{10,9... | collective-permute-start | bytes 1179656 | tf_op jit(solution)/shard_map/ppermute | solution.py:23
  278.4 8.4 %collective-permute-start.6 = (bf16[2,256,384]{2,1,0:T(8,128)(2,1)S(1)}, bf16[2,256,384]{2,1,0:T(8,128)(2,1)S(1)}, u32[]{:S(2)}, u32[]{:S(2)}) collective-permute-start(bf16[2,256,384]{2,1,0:T(8,128)(2,1)S(1)} %collective-permute-done.4), channel_id=1, source_target_pairs={{0,1},{1,2},{2,3},{3,4},{4,5},{5,6},{6,7},{7,8},{8,9},{9,10},{10,1... | collective-permute-start | bytes 1179656 | tf_op jit(solution)/shard_map/ppermute | solution.py:18
  278.6 9.3 %collective-permute-start.7 = (bf16[2,256,384]{2,1,0:T(8,128)(2,1)S(1)}, bf16[2,256,384]{2,1,0:T(8,128)(2,1)S(1)}, u32[]{:S(2)}, u32[]{:S(2)}) collective-permute-start(bf16[2,256,384]{2,1,0:T(8,128)(2,1)S(1)} %collective-permute-done.5), channel_id=1, source_target_pairs={{0,15},{1,0},{2,1},{3,2},{4,3},{5,4},{6,5},{7,6},{8,7},{9,8},{10,9... | collective-permute-start | bytes 1179656 | tf_op jit(solution)/shard_map/ppermute | solution.py:23
  286.9 8.4 %collective-permute-start.8 = (bf16[2,256,384]{2,1,0:T(8,128)(2,1)S(1)}, bf16[2,256,384]{2,1,0:T(8,128)(2,1)S(1)}, u32[]{:S(2)}, u32[]{:S(2)}) collective-permute-start(bf16[2,256,384]{2,1,0:T(8,128)(2,1)S(1)} %collective-permute-done.6), channel_id=1, source_target_pairs={{0,1},{1,2},{2,3},{3,4},{4,5},{5,6},{6,7},{7,8},{8,9},{9,10},{10,1... | collective-permute-start | bytes 1179656 | tf_op jit(solution)/shard_map/ppermute | solution.py:18
  286.9 1.0 copy-start.1
  287.9 8.6 %collective-permute-start.9 = (bf16[2,256,384]{2,1,0:T(8,128)(2,1)S(1)}, bf16[2,256,384]{2,1,0:T(8,128)(2,1)S(1)}, u32[]{:S(2)}, u32[]{:S(2)}) collective-permute-start(bf16[2,256,384]{2,1,0:T(8,128)(2,1)S(1)} %collective-permute-done.7), channel_id=1, source_target_pairs={{0,15},{1,0},{2,1},{3,2},{4,3},{5,4},{6,5},{7,6},{8,7},{9,8},{10,9... | collective-permute-start | bytes 1179656 | tf_op jit(solution)/shard_map/ppermute | solution.py:23
  295.3 8.4 %collective-permute-start.10 = (bf16[2,256,384]{2,1,0:T(8,128)(2,1)S(1)}, bf16[2,256,384]{2,1,0:T(8,128)(2,1)S(1)}, u32[]{:S(2)}, u32[]{:S(2)}) collective-permute-start(bf16[2,256,384]{2,1,0:T(8,128)(2,1)S(1)} %collective-permute-done.8), channel_id=1, source_target_pairs={{0,1},{1,2},{2,3},{3,4},{4,5},{5,6},{6,7},{7,8},{8,9},{9,10},{10,1... | collective-permute-start | bytes 1179656 | tf_op jit(solution)/shard_map/ppermute | solution.py:18
  296.5 8.2 %collective-permute-start.11 = (bf16[2,256,384]{2,1,0:T(8,128)(2,1)S(1)}, bf16[2,256,384]{2,1,0:T(8,128)(2,1)S(1)}, u32[]{:S(2)}, u32[]{:S(2)}) collective-permute-start(bf16[2,256,384]{2,1,0:T(8,128)(2,1)S(1)} %collective-permute-done.9), channel_id=1, source_target_pairs={{0,15},{1,0},{2,1},{3,2},{4,3},{5,4},{6,5},{7,6},{8,7},{9,8},{10,9... | collective-permute-start | bytes 1179656 | tf_op jit(solution)/shard_map/ppermute | solution.py:23
  303.7 8.4 %collective-permute-start.12 = (bf16[2,256,384]{2,1,0:T(8,128)(2,1)S(1)}, bf16[2,256,384]{2,1,0:T(8,128)(2,1)S(1)}, u32[]{:S(2)}, u32[]{:S(2)}) collective-permute-start(bf16[2,256,384]{2,1,0:T(8,128)(2,1)S(1)} %collective-permute-done.10), channel_id=1, source_target_pairs={{0,1},{1,2},{2,3},{3,4},{4,5},{5,6},{6,7},{7,8},{8,9},{9,10},{10,1... | collective-permute-start | bytes 1179656 | tf_op jit(solution)/shard_map/ppermute | solution.py:18
  304.7 8.4 %collective-permute-start.13 = (bf16[2,256,384]{2,1,0:T(8,128)(2,1)S(1)}, bf16[2,256,384]{2,1,0:T(8,128)(2,1)S(1)}, u32[]{:S(2)}, u32[]{:S(2)}) collective-permute-start(bf16[2,256,384]{2,1,0:T(8,128)(2,1)S(1)} %collective-permute-done.11), channel_id=1, source_target_pairs={{0,15},{1,0},{2,1},{3,2},{4,3},{5,4},{6,5},{7,6},{8,7},{9,8},{10,9... | collective-permute-start | bytes 1179656 | tf_op jit(solution)/shard_map/ppermute | solution.py:23
  312.1 8.4 %collective-permute-start.14 = (bf16[2,256,384]{2,1,0:T(8,128)(2,1)S(1)}, bf16[2,256,384]{2,1,0:T(8,128)(2,1)S(1)}, u32[]{:S(2)}, u32[]{:S(2)}) collective-permute-start(bf16[2,256,384]{2,1,0:T(8,128)(2,1)S(1)} %collective-permute-done.12), channel_id=1, source_target_pairs={{0,1},{1,2},{2,3},{3,4},{4,5},{5,6},{6,7},{7,8},{8,9},{9,10},{10,1... | collective-permute-start | bytes 1179656 | tf_op jit(solution)/shard_map/ppermute | solution.py:18
Sparse Core Ops, SparseCore 0:
  9.2 45.1 all-gather.1
  324.6 143.0 all-reduce.1
